TPU v7x, 256 devices: a whole 4x4x8 slice. The times are simulated.
256 devices in a mesh: group: 8 (over x, core), dom: 32 (over y, z).
Axes of the slice: x: 4, y: 4, z: 8, core: 2. Of those that a mesh axis runs over, the one named last changes fastest.
Arguments:
- flow_state: float32 [5, 1048576], P(None, ('group', 'dom')), may hold values from -6 to 6
- right_side: float32 [5, 1048576], P(None, ('group', 'dom')), may hold values from -6 to 6
- coupling: float32 [1048576], P(('group', 'dom')), may hold values from 0.03 to 0.3
- pivot_inv: float32 [32, 25, 32768], P(None, None, ('group', 'dom'))
- lower_blocks: float32 [32, 25, 32768], P(None, None, ('group', 'dom'))
- upper_blocks: float32 [32, 25, 32768], P(None, None, ('group', 'dom')), may hold values from -0.15 to 0.15
- face_up: int32 [8, 32, 256], P('group', 'dom'), may hold values from 0 to 4095, as said below
- face_down: int32 [8, 32, 256], P('group', 'dom'), may hold values from 0 to 4095, as said below
- coef_up: float32 [8, 32, 256], P('group', 'dom'), may hold values from 0.1 to 0.5
- coef_down: float32 [8, 32, 256], P('group', 'dom'), may hold values from 0.1 to 0.5
- send_cell: int32 [32, 32768], P(None, ('group', 'dom')), may hold values from 0 to 4095, as said below
- line_src: int32 [32, 32768], P(None, ('group', 'dom')), may hold values from 0 to 8191, as said below
- ret_slot: int32 [32, 32768], P(None, ('group', 'dom')), may hold values from 0 to 4095, as said below
- cell_src: int32 [1048576], P(('group', 'dom')), may hold values from 0 to 8191, as said below
Outputs:
- solution: float32 [5, 1048576], P(None, ('group', 'dom'))
- drive_next: float32 [5, 1048576], P(None, ('group', 'dom'))
Inputs may be any that keep to these rules, and one draw needn't show every extreme that they name: Within a group, the cells named by send_cell for all owners together with the own cells named by line_src cover every cell exactly once; for each sender and owner, the first entries, as many as the cells that sender sends that owner (at most 128), are used and the rest are unused; at most 128 cells go from one partition to one other owner, and this is reached for many pairs in every draw; a partition sends none of its cells to itself through send_cell. `ret_slot`: used entries point at the slot that holds the sent cell. `cell_src`: each cell's value returns to it from the slot that took it. `face_up`: distinct cells within one partition's list. `face_down`: distinct cells within one partition's list.
All inputs are finite; a program needn't handle non-finite values.
Results may differ from a plain program's by a relative error of at most 0.0001.
Values sent between devices are 32-bit elements; how exact they have to be, the bound alone decides.
A program may use at most 192 MiB of HBM per device.

v0:
```python
import jax
import jax.numpy as jnp
from jax import lax
from jax.sharding import PartitionSpec as P

SWEEPS = 2


def shifted(block, axis, distance):
    devices = range(lax.axis_size(axis))
    route = [(i - distance, i) for i in devices if i - distance in devices]
    return lax.ppermute(block, axis, route)


def apply_block(matrix, vector):
    nvar = vector.shape[0]
    return jnp.sum(matrix.reshape(nvar, nvar, -1) * vector[None, :, :], axis=1)


def solve_lines(line_vals, pivot_inv, lower_blocks, upper_blocks):
    nvar = line_vals.shape[0]
    line_len, _, line_count = pivot_inv.shape
    blocks = line_vals.reshape(nvar, line_len, line_count)
    forward_vals = []
    previous = None
    for cell_position in range(line_len):
        reduced = blocks[:, cell_position]
        if cell_position > 0:
            reduced = reduced - apply_block(lower_blocks[cell_position], previous)
        previous = apply_block(pivot_inv[cell_position], reduced)
        forward_vals.append(previous)
    results = [None] * line_len
    later = forward_vals[-1]
    results[-1] = later
    for cell_position in range(line_len - 2, -1, -1):
        later = forward_vals[cell_position] - apply_block(upper_blocks[cell_position], later)
        results[cell_position] = later
    return jnp.stack(results, axis=1).reshape(nvar, line_len * line_count)


def shards(
    flow_state,
    right_side,
    coupling,
    pivot_inv,
    lower_blocks,
    upper_blocks,
    face_up,
    face_down,
    coef_up,
    coef_down,
    send_cell,
    line_src,
    ret_slot,
    cell_src,
):
    nvar = flow_state.shape[0]
    cell_count = flow_state.shape[1]
    domains = lax.axis_size("dom")
    capacity = send_cell.shape[1]
    pool_base = domains * capacity
    up_cells = face_up.reshape(-1)
    down_cells = face_down.reshape(-1)
    up_coef = coef_up.reshape(-1)
    down_coef = coef_down.reshape(-1)
    slot_map = line_src.reshape(-1)

    def drive_term(values):
        zeros_col = jnp.zeros((nvar, 1), jnp.float32)
        beside = jnp.concatenate([zeros_col, values[:, :-1]], 1) + jnp.concatenate(
            [values[:, 1:], zeros_col], 1
        )
        total = right_side + coupling[None, :] * beside
        up_vals = values[:, up_cells]
        down_vals = values[:, down_cells]
        from_below = shifted(up_vals, "group", 1)
        from_above = shifted(down_vals, "group", -1)
        total = total.at[:, down_cells].add(down_coef[None, :] * from_below)
        total = total.at[:, up_cells].add(up_coef[None, :] * from_above)
        return total

    peer_maps = lax.all_to_all(send_cell, "dom", split_axis=0, concat_axis=0, tiled=True)
    remote = slot_map < pool_base
    clipped = jnp.minimum(slot_map, pool_base - 1)
    global_idx = clipped // capacity * cell_count + peer_maps.reshape(-1)[clipped]
    own_idx = jnp.clip(slot_map - pool_base, 0, cell_count - 1)
    state_now = flow_state
    for sweep_idx in range(SWEEPS):
        drive_vals = drive_term(state_now)
        whole = lax.all_gather(drive_vals, "dom", axis=1, tiled=True)
        line_vals = jnp.where(remote[None, :], whole[:, global_idx], drive_vals[:, own_idx])
        solved = solve_lines(line_vals, pivot_inv, lower_blocks, upper_blocks)
        outgoing = solved[:, ret_slot]
        returned = lax.all_to_all(outgoing, "dom", split_axis=1, concat_axis=1, tiled=True)
        pooled = jnp.concatenate([returned.reshape(nvar, pool_base), solved], 1)
        state_now = pooled[:, cell_src]
    drive_last = drive_term(state_now)
    return (state_now, drive_last)


def solution(mesh):
    return jax.shard_map(
        shards,
        mesh=mesh,
        in_specs=(
            P(None, ("group", "dom")),
            P(None, ("group", "dom")),
            P(("group", "dom")),
            P(None, None, ("group", "dom")),
            P(None, None, ("group", "dom")),
            P(None, None, ("group", "dom")),
            P("group", "dom", None),
            P("group", "dom", None),
            P("group", "dom", None),
            P("group", "dom", None),
            P(None, ("group", "dom")),
            P(None, ("group", "dom")),
            P(None, ("group", "dom")),
            P(("group", "dom")),
        ),
        out_specs=(P(None, ("group", "dom")), P(None, ("group", "dom"))),
        check_vma=False,
    )
```

profile of v0, /device:TPU:1, one launch (start us, length us, event | category | flops | bytes accessed | tf_op | source)
XLA Modules:
  0.0 1229.4 jit_solution(4603384156076529335)
XLA Ops:
  11.0 4.5 collective-permute-start
  26.7 11.2 all-to-all-start
  40.2 3.4 slice_reduce_fusion.2
  95.0 14.1 %gather_fusion.4 = f32[4096,5]{1,0:T(8,128)} fusion(f32[5,4096]{0,1:T(8,128)S(1)} %copy-done.1, s32[4096]{0:T(1024)S(1)} %broadcast_clamp_fusion.1), kind=kCustom, calls=%fused_computation.4 | custom fusion | bytes 180224 | tf_op jit(solution)/shard_map/gather | solution.py:91
  111.2 23.2 %gather_fusion.2 = s32[4096]{0:T(1024)S(1)} fusion(s32[4096]{0:T(1024)S(1)} %bitcast.448, s32[4096]{0:T(1024)} %broadcast_clamp_fusion.2), kind=kCustom, calls=%fused_computation.2 | custom fusion | bytes 49152 | tf_op jit(solution)/shard_map/gather | solution.py:85
  134.5 325.0 %all-gather.3.cloned.1.call-done = f32[5,131072]{0,1:T(8,128)} async-done(((f32[5,4096]{0,1:T(8,128)}), f32[5,131072]{0,1:T(8,128)}) %all-gather.3.cloned.1.call-update) | async-done | bytes 2621456 | tf_op jit(solution)/shard_map/all_gather | solution.py:90
  459.5 62.3 %gather_fusion.3 = f32[4096,5]{1,0:T(8,128)S(1)} fusion(f32[5,131072]{0,1:T(8,128)} %all-gather.3.cloned.1.call-done, s32[4096]{0:T(1024)S(1)} %broadcast_clamp_fusion), kind=kCustom, calls=%fused_computation.3 | custom fusion | bytes 180224 | tf_op jit(solution)/shard_map/gather | solution.py:91
  557.4 14.1 %gather_fusion.5 = f32[4096,5]{1,0:T(8,128)} fusion(f32[5,4096]{0,1:T(8,128)S(1)} %bitcast.451, s32[4096]{0:T(1024)S(1)} %copy-done.17), kind=kCustom, calls=%fused_computation.5 | custom fusion | bytes 180224 | tf_op jit(solution)/shard_map/gather | solution.py:93
  573.7 15.9 %all_to_all.19 = f32[5,32,128]{2,0,1:T(8,128)S(1)} all-to-all(f32[5,32,128]{2,0,1:T(8,128)S(1)} %bitcast.468), channel_id=1, replica_groups=mesh['group'=8,'dom'=32] {'dom'}, dimensions={1} | all-to-all | bytes 163840 | tf_op jit(solution)/shard_map/all_to_all | solution.py:94
  591.5 3.8 pad_maximum_fusion
  595.3 13.0 %gather_fusion.6 = f32[4096,5]{1,0:T(8,128)S(1)} fusion(f32[5,8192]{0,1:T(8,128)} %pad_maximum_fusion, s32[4096]{0:T(1024)S(1)} %copy-done.12), kind=kCustom, calls=%fused_computation.6 | custom fusion | bytes 180224 | tf_op jit(solution)/shard_map/gather | solution.py:96
  612.1 5.9 collective-permute-start.2
  621.0 3.2 scatter_custom_fusion.2
  624.7 3.1 scatter_custom_fusion.3
  629.2 12.4 %gather_fusion.10 = f32[4096,5]{1,0:T(8,128)S(1)} fusion(f32[5,4096]{0,1:T(8,128)} %copy-done.2, s32[4096]{0:T(1024)S(1)} %copy-done.9), kind=kCustom, calls=%fused_computation.10 | custom fusion | bytes 180224 | tf_op jit(solution)/shard_map/gather | solution.py:91
  642.2 412.6 %all-gather.5.cloned.1.call-done = f32[5,131072]{0,1:T(8,128)} async-done(((f32[5,4096]{0,1:T(8,128)}), f32[5,131072]{0,1:T(8,128)}) %all-gather.5.cloned.1.call-update) | async-done | bytes 2621456 | tf_op jit(solution)/shard_map/all_gather | solution.py:90
  1054.8 62.3 %gather_fusion.9 = f32[4096,5]{1,0:T(8,128)S(1)} fusion(f32[5,131072]{0,1:T(8,128)} %all-gather.5.cloned.1.call-done, s32[4096]{0:T(1024)S(1)} %copy-done.11), kind=kCustom, calls=%fused_computation.9 | custom fusion | bytes 180224 | tf_op jit(solution)/shard_map/gather | solution.py:91
  1152.6 14.1 %gather_fusion.11 = f32[4096,5]{1,0:T(8,128)} fusion(f32[5,4096]{0,1:T(8,128)S(1)} %bitcast.449, s32[4096]{0:T(1024)S(1)} %copy-done.18), kind=kCustom, calls=%fused_computation.11 | custom fusion | bytes 180224 | tf_op jit(solution)/shard_map/gather | solution.py:93
  1168.9 15.9 %all_to_all.20 = f32[5,32,128]{2,0,1:T(8,128)S(1)} all-to-all(f32[5,32,128]{2,0,1:T(8,128)S(1)} %bitcast.469), channel_id=1, replica_groups=mesh['group'=8,'dom'=32] {'dom'}, dimensions={1} | all-to-all | bytes 163840 | tf_op jit(solution)/shard_map/all_to_all | solution.py:94
  1186.8 3.8 pad_maximum_fusion.1
  1190.6 13.0 %gather_fusion.12 = f32[4096,5]{1,0:T(8,128)S(1)} fusion(f32[5,8192]{0,1:T(8,128)} %pad_maximum_fusion.1, s32[4096]{0:T(1024)S(1)} %copy-done.13), kind=kCustom, calls=%fused_computation.12 | custom fusion | bytes 180224 | tf_op jit(solution)/shard_map/gather | solution.py:96
  1206.1 5.9 collective-permute-start.4
  1214.8 2.9 scatter_custom_fusion.4
  1218.4 2.9 scatter_custom_fusion.5
  (638 shorter events, 163.4 us)
Async XLA Ops:
  7.2 452.3 %all-gather.3.cloned.1.call-start = ((), (), s32[]{:S(2)}) async-start(), calls=%async_computation.3 | async-start | bytes 69206016 | tf_op jit(solution)/shard_map/all_gather | solution.py:90
  11.0 8.1 collective-permute-start
  16.2 6.3 collective-permute-start.1
  26.7 84.6 %all-to-all-start = ((s32[32,1,128]{2,1,0:T(1,128)}), s32[32,1,128]{2,1,0:T(1,128)S(1)}, u32[]{:S(2)}, u32[]{:S(2)}) async-start(s32[32,1,128]{2,1,0:T(1,128)} %bitcast.11), calls=%async_computation | async-start | bytes 32768 | tf_op jit(solution)/shard_map/all_to_all | solution.py:82
  37.9 1016.9 %all-gather.5.cloned.1.call-start = ((), (), s32[]{:S(2)}) async-start(), calls=%async_computation.4 | async-start | bytes 69206016 | tf_op jit(solution)/shard_map/all_gather | solution.py:90
  44.8 49.7 %copy-start.32 = (f32[25,128]{1,0:T(8,128)S(1)}, f32[25,128]{1,0:T(8,128)}, u32[]{:S(2)}) copy-start(f32[25,128]{1,0:T(8,128)} %get-tuple-element.51) | copy-start | bytes 38404
  44.8 49.7 %copy-start.31 = (f32[25,128]{1,0:T(8,128)S(1)}, f32[25,128]{1,0:T(8,128)}, u32[]{:S(2)}) copy-start(f32[25,128]{1,0:T(8,128)} %get-tuple-element.52) | copy-start | bytes 38404
  44.8 49.7 %copy-start.29 = (f32[25,128]{1,0:T(8,128)S(1)}, f32[25,128]{1,0:T(8,128)}, u32[]{:S(2)}) copy-start(f32[25,128]{1,0:T(8,128)} %get-tuple-element.53) | copy-start | bytes 38404
  44.9 49.7 %copy-start.28 = (f32[25,128]{1,0:T(8,128)S(1)}, f32[25,128]{1,0:T(8,128)}, u32[]{:S(2)}) copy-start(f32[25,128]{1,0:T(8,128)} %get-tuple-element.54) | copy-start | bytes 38404
  44.9 49.7 %copy-start.27 = (f32[25,128]{1,0:T(8,128)S(1)}, f32[25,128]{1,0:T(8,128)}, u32[]{:S(2)}) copy-start(f32[25,128]{1,0:T(8,128)} %get-tuple-element.55) | copy-start | bytes 38404
  44.9 49.7 %copy-start.26 = (f32[25,128]{1,0:T(8,128)S(1)}, f32[25,128]{1,0:T(8,128)}, u32[]{:S(2)}) copy-start(f32[25,128]{1,0:T(8,128)} %get-tuple-element.56) | copy-start | bytes 38404
  44.9 49.7 %copy-start.25 = (f32[25,128]{1,0:T(8,128)S(1)}, f32[25,128]{1,0:T(8,128)}, u32[]{:S(2)}) copy-start(f32[25,128]{1,0:T(8,128)} %get-tuple-element.57) | copy-start | bytes 38404
  44.9 49.7 %copy-start.24 = (f32[25,128]{1,0:T(8,128)S(1)}, f32[25,128]{1,0:T(8,128)}, u32[]{:S(2)}) copy-start(f32[25,128]{1,0:T(8,128)} %get-tuple-element.58) | copy-start | bytes 38404
  44.9 49.8 %copy-start.23 = (f32[25,128]{1,0:T(8,128)S(1)}, f32[25,128]{1,0:T(8,128)}, u32[]{:S(2)}) copy-start(f32[25,128]{1,0:T(8,128)} %get-tuple-element.59) | copy-start | bytes 38404
  44.9 49.8 %copy-start.22 = (f32[25,128]{1,0:T(8,128)S(1)}, f32[25,128]{1,0:T(8,128)}, u32[]{:S(2)}) copy-start(f32[25,128]{1,0:T(8,128)} %get-tuple-element.60) | copy-start | bytes 38404
  44.9 49.8 %copy-start.21 = (f32[25,128]{1,0:T(8,128)S(1)}, f32[25,128]{1,0:T(8,128)}, u32[]{:S(2)}) copy-start(f32[25,128]{1,0:T(8,128)} %get-tuple-element.61) | copy-start | bytes 38404
  44.9 49.8 %copy-start.20 = (f32[25,128]{1,0:T(8,128)S(1)}, f32[25,128]{1,0:T(8,128)}, u32[]{:S(2)}) copy-start(f32[25,128]{1,0:T(8,128)} %get-tuple-element.62) | copy-start | bytes 38404
  47.5 61.5 %copy-start.8 = (s32[4096]{0:T(1024)}, s32[4096]{0:T(1024)S(1)}, u32[]{:S(2)}) copy-start(s32[4096]{0:T(1024)S(1)} %broadcast_clamp_fusion.1) | copy-start | bytes 49156
  134.5 387.3 %copy-start.10 = (s32[4096]{0:T(1024)}, s32[4096]{0:T(1024)S(1)}, u32[]{:S(2)}) copy-start(s32[4096]{0:T(1024)S(1)} %broadcast_clamp_fusion) | copy-start | bytes 49156
  612.1 8.9 collective-permute-start.2
  618.1 6.6 collective-permute-start.3
  629.2 425.6 %copy-start.11 = (s32[4096]{0:T(1024)S(1)}, s32[4096]{0:T(1024)}, u32[]{:S(2)}) copy-start(s32[4096]{0:T(1024)} %copy-done.10) | copy-start | bytes 49156
  1206.1 8.7 collective-permute-start.4
  1212.1 6.3 collective-permute-start.5
  (37 other events, 775.1 us)
Sparse Core Ops, SparseCore 0:
  26.8 432.6 all-gather.2
  629.3 425.4 all-gather.4
where the time goes:
time: 1240 us; the launch traced here: 1230 us
  waiting for transfers between devices  739 us (60%)
  local copies, waits for them, and re-layouts  311 us (25%)
  other arithmetic  95.7 us (8%)
  starting transfers between devices  33.8 us (3%)
  blocking collectives  31.8 us (3%)
  between operations  17.7 us (1%)
    all_gather x2, waiting for transfers between devices, shards(): whole = lax.all_gather(drive_vals, 'dom', axis=1, tiled=True)  738 us
    gather x4, local copies, waits for them, and re-layouts, shards(): whole[:, global_idx]  126 us
    reduce_sum x188, other arithmetic, apply_block(): return jnp.sum(matrix.reshape(nvar, nvar, -1) * vector[None, :, :], axis=1)  63.9 us
    another operation x94, local copies, waits for them, and re-layouts, apply_block(): return jnp.sum(matrix.reshape(nvar, nvar, -1) * vector[None, :, :], axis=1)  43.4 us
    gather x4, local copies, waits for them, and re-layouts, shards(): outgoing = solved[:, ret_slot]  32.6 us
    all_to_all x2, blocking collectives, shards(): lax.all_to_all(outgoing, 'dom', split_axis=1, concat_axis=1, tiled=True)  31.8 us
    gather x4, local copies, waits for them, and re-layouts, shards(): drive_vals[:, own_idx]  29.3 us
    gather x4, local copies, waits for them, and re-layouts, shards(): state_now = pooled[:, cell_src]  27.2 us
  transfers between devices with their start and end apart: 9, of which 5 were waited for; matrix products, arithmetic and copies ran while one was open for 10% of the time, Pallas kernels for 0%

commit v1 on v0

--- a/solution.py
+++ b/solution.py
@@ -2,6 +2,7 @@
 import jax.numpy as jnp
 from jax import lax
 from jax.sharding import PartitionSpec as P
+from jax.lax import all_to_all, axis_size
 
 SWEEPS = 2
 
@@ -87,7 +88,19 @@
     state_now = flow_state
     for sweep_idx in range(SWEEPS):
         drive_vals = drive_term(state_now)
-        whole = lax.all_gather(drive_vals, "dom", axis=1, tiled=True)
+
+        def divide_outputs_by_axis(z):
+            return jnp.concatenate(
+                all_to_all(
+                    jnp.stack(tuple((z for _ in range(axis_size("dom"))))),
+                    axis_name="dom",
+                    split_axis=0,
+                    concat_axis=0,
+                ),
+                axis=1,
+            )
+
+        whole = divide_outputs_by_axis(drive_vals)
         line_vals = jnp.where(remote[None, :], whole[:, global_idx], drive_vals[:, own_idx])
         solved = solve_lines(line_vals, pivot_inv, lower_blocks, upper_blocks)
         outgoing = solved[:, ret_slot]

time: 1240 us -> 641 us (0.52)
  waiting for transfers between devices: 739 us -> 80.5 us
  local copies, waits for them, and re-layouts: 311 us -> 377 us
  starting transfers between devices: 33.8 us -> 51.3 us
  between operations: 17.7 us -> 4.22 us
    all_gather x2 -> x0, waiting for transfers between devices: 738 us -> none  [shards(): whole = lax.all_gather(drive_vals, 'dom', axis=1, tiled=True)]
    all_to_all x0 -> x2, waiting for transfers between devices: none -> 76.9 us  [divide_outputs_by_axis(): all_to_all(jnp.stack(tuple((z for _ in range(axis_size('dom'))))), axis_n...]
    reshape x0 -> x2, local copies, waits for them, and re-layouts: none -> 61.1 us  [divide_outputs_by_axis(): jnp.concatenate(all_to_all(jnp.stack(tuple((z for _ in range(axis_size('d...]
    all_to_all x0 -> x2, starting transfers between devices: none -> 14.8 us  [divide_outputs_by_axis(): all_to_all(jnp.stack(tuple((z for _ in range(axis_size('dom'))))), axis_n...]
  transfers between devices with their start and end apart: 9 -> 9, of which waited for: 5 -> 5; matrix products, arithmetic and copies ran while one was open for 10% -> 20% of each run, Pallas kernels for 0% -> 0%
where the time goes in v1:
time: 641 us; the launch traced here: 633 us
  local copies, waits for them, and re-layouts  377 us (59%)
  other arithmetic  84.7 us (13%)
  waiting for transfers between devices  80.5 us (13%)
  starting transfers between devices  51.3 us (8%)
  blocking collectives  34.8 us (5%)
    gather x4, local copies, waits for them, and re-layouts, shards(): whole[:, global_idx]  126 us
    all_to_all x2, waiting for transfers between devices, divide_outputs_by_axis(): all_to_all(jnp.stack(tuple((z for _ in range(axis_size('dom'))))), axis_n...  76.9 us
    reshape x2, local copies, waits for them, and re-layouts, divide_outputs_by_axis(): jnp.concatenate(all_to_all(jnp.stack(tuple((z for _ in range(axis_size('d...  61.1 us
    reduce_sum x188, other arithmetic, apply_block(): return jnp.sum(matrix.reshape(nvar, nvar, -1) * vector[None, :, :], axis=1)  55.3 us
    another operation x94, local copies, waits for them, and re-layouts, apply_block(): return jnp.sum(matrix.reshape(nvar, nvar, -1) * vector[None, :, :], axis=1)  44.3 us
    all_to_all x2, blocking collectives, shards(): lax.all_to_all(outgoing, 'dom', split_axis=1, concat_axis=1, tiled=True)  34.8 us
    gather x4, local copies, waits for them, and re-layouts, shards(): outgoing = solved[:, ret_slot]  32.6 us
    gather x4, local copies, waits for them, and re-layouts, shards(): drive_vals[:, own_idx]  32.6 us
  transfers between devices with their start and end apart: 9, of which 5 were waited for; matrix products, arithmetic and copies ran while one was open for 20% of the time, Pallas kernels for 0%

profile of v1, /device:TPU:1, one launch (start us, length us, event | category | flops | bytes accessed | tf_op | source)
XLA Modules:
  0.0 632.7 jit_solution(10102585403178020536)
XLA Ops:
  0.7 12.2 %all-to-all-start.1 = ((s32[32,1,128]{2,1,0:T(1,128)}), s32[32,1,128]{2,1,0:T(1,128)S(1)}, u32[]{:S(2)}, u32[]{:S(2)}) async-start(s32[32,1,128]{2,1,0:T(1,128)} %bitcast.481), calls=%async_computation.1 | async-start | bytes 32768 | tf_op jit(solution)/shard_map/all_to_all | solution.py:83
  33.7 9.9 %all-to-all-start = ((f32[32,5,4096]{2,1,0:T(8,128)}), f32[32,5,4096]{2,1,0:T(8,128)}, u32[]{:S(2)}, u32[]{:S(2)}) async-start(f32[32,5,4096]{2,1,0:T(8,128)} %stack.12), calls=%async_computation | async-start | bytes 8388608 | tf_op jit(solution)/shard_map/all_to_all | solution.py:94
  98.2 14.1 %gather_fusion.4 = f32[4096,5]{1,0:T(8,128)} fusion(f32[5,4096]{0,1:T(8,128)S(1)} %scatter_custom_fusion.1, s32[4096]{0:T(1024)S(1)} %broadcast_clamp_fusion.1), kind=kCustom, calls=%fused_computation.4 | custom fusion | bytes 180224 | tf_op jit(solution)/shard_map/gather | solution.py:104
  114.4 23.0 %gather_fusion.2 = s32[4096]{0:T(1024)S(1)} fusion(s32[4096]{0:T(1024)S(1)} %bitcast.452, s32[4096]{0:T(1024)S(1)} %broadcast_clamp_fusion.2), kind=kCustom, calls=%fused_computation.2 | custom fusion | bytes 49152 | tf_op jit(solution)/shard_map/gather | solution.py:86
  137.7 30.5 %copy.526 = f32[5,32,4096]{0,2,1:T(8,128)} copy(f32[5,32,4096]{2,0,1:T(8,128)} %bitcast.10) | data formatting | bytes 5242880 | tf_op jit(solution)/shard_map/reshape | solution.py:93
  168.3 62.3 %gather_fusion.3 = f32[4096,5]{1,0:T(8,128)S(1)} fusion(f32[5,131072]{0,1:T(8,128)} %bitcast.11, s32[4096]{0:T(1024)S(1)} %broadcast_clamp_fusion), kind=kCustom, calls=%fused_computation.3 | custom fusion | bytes 180224 | tf_op jit(solution)/shard_map/gather | solution.py:104
  261.3 14.1 %gather_fusion.5 = f32[4096,5]{1,0:T(8,128)} fusion(f32[5,4096]{0,1:T(8,128)S(1)} %bitcast.455, s32[4096]{0:T(1024)S(1)} %copy-done.37), kind=kCustom, calls=%fused_computation.5 | custom fusion | bytes 180224 | tf_op jit(solution)/shard_map/gather | solution.py:106
  277.6 20.0 %all_to_all.29 = f32[5,32,128]{2,0,1:T(8,128)S(1)} all-to-all(f32[5,32,128]{2,0,1:T(8,128)S(1)} %bitcast.472), channel_id=1, replica_groups=mesh['group'=8,'dom'=32] {'dom'}, dimensions={1} | all-to-all | bytes 163840 | tf_op jit(solution)/shard_map/all_to_all | solution.py:107
  299.6 3.8 pad_maximum_fusion
  303.4 13.0 %gather_fusion.6 = f32[4096,5]{1,0:T(8,128)S(1)} fusion(f32[5,8192]{0,1:T(8,128)} %pad_maximum_fusion, s32[4096]{0:T(1024)S(1)} %copy-done.32), kind=kCustom, calls=%fused_computation.6 | custom fusion | bytes 180224 | tf_op jit(solution)/shard_map/gather | solution.py:109
  321.9 6.3 collective-permute-start.2
  330.5 3.1 scatter_custom_fusion.2
  333.6 3.2 scatter_custom_fusion.3
  339.8 4.9 all-to-all-start.3
  344.7 14.1 %gather_fusion.10 = f32[4096,5]{1,0:T(8,128)} fusion(f32[5,4096]{0,1:T(8,128)S(1)} %scatter_custom_fusion.3, s32[4096]{0:T(1024)S(1)} %broadcast_clamp_fusion.1), kind=kCustom, calls=%fused_computation.10 | custom fusion | bytes 180224 | tf_op jit(solution)/shard_map/gather | solution.py:104
  361.0 76.9 %all-to-all-done.3 = f32[32,5,4096]{2,1,0:T(8,128)} async-done(((f32[32,5,4096]{2,1,0:T(8,128)}), f32[32,5,4096]{2,1,0:T(8,128)}, u32[]{:S(2)}, u32[]{:S(2)}) %all-to-all-start.3) | async-done | bytes 2621472 | tf_op jit(solution)/shard_map/all_to_all | solution.py:94
  437.9 30.6 %copy.537 = f32[5,32,4096]{0,2,1:T(8,128)} copy(f32[5,32,4096]{2,0,1:T(8,128)} %bitcast.99) | data formatting | bytes 5242880 | tf_op jit(solution)/shard_map/reshape | solution.py:93
  468.4 62.3 %gather_fusion.9 = f32[4096,5]{1,0:T(8,128)S(1)} fusion(f32[5,131072]{0,1:T(8,128)} %bitcast.100, s32[4096]{0:T(1024)S(1)} %copy-done.31), kind=kCustom, calls=%fused_computation.9 | custom fusion | bytes 180224 | tf_op jit(solution)/shard_map/gather | solution.py:104
  561.4 14.1 %gather_fusion.11 = f32[4096,5]{1,0:T(8,128)} fusion(f32[5,4096]{0,1:T(8,128)S(1)} %bitcast.453, s32[4096]{0:T(1024)S(1)} %copy-done.38), kind=kCustom, calls=%fused_computation.11 | custom fusion | bytes 180224 | tf_op jit(solution)/shard_map/gather | solution.py:106
  577.6 14.8 %all_to_all.30 = f32[5,32,128]{2,0,1:T(8,128)S(1)} all-to-all(f32[5,32,128]{2,0,1:T(8,128)S(1)} %bitcast.473), channel_id=1, replica_groups=mesh['group'=8,'dom'=32] {'dom'}, dimensions={1} | all-to-all | bytes 163840 | tf_op jit(solution)/shard_map/all_to_all | solution.py:107
  594.4 3.8 pad_maximum_fusion.1
  598.2 13.0 %gather_fusion.12 = f32[4096,5]{1,0:T(8,128)S(1)} fusion(f32[5,8192]{0,1:T(8,128)} %pad_maximum_fusion.1, s32[4096]{0:T(1024)S(1)} %copy-done.33), kind=kCustom, calls=%fused_computation.12 | custom fusion | bytes 180224 | tf_op jit(solution)/shard_map/gather | solution.py:109
  615.6 7.8 %collective-permute-start.4 = (f32[5,256]{0,1:T(8,128)S(1)}, f32[5,256]{0,1:T(8,128)S(1)}, u32[]{:S(2)}, u32[]{:S(2)}) collective-permute-start(f32[5,256]{0,1:T(8,128)S(1)} %bitcast.499), channel_id=1, source_target_pairs={{0,32},{32,64},{64,96},{96,128},{128,160},{160,192},{192,224},{1,3... | collective-permute-start | bytes 15368 | tf_op jit(solution)/shard_map/ppermute | solution.py:13
  625.3 3.2 scatter_custom_fusion.4
  (630 shorter events, 167.8 us)
Async XLA Ops:
  0.7 30.6 %all-to-all-start.1 = ((s32[32,1,128]{2,1,0:T(1,128)}), s32[32,1,128]{2,1,0:T(1,128)S(1)}, u32[]{:S(2)}, u32[]{:S(2)}) async-start(s32[32,1,128]{2,1,0:T(1,128)} %bitcast.481), calls=%async_computation.1 | async-start | bytes 32768 | tf_op jit(solution)/shard_map/all_to_all | solution.py:83
  16.5 11.3 %collective-permute-start.1 = (f32[5,256]{0,1:T(8,128)S(1)}, f32[5,256]{0,1:T(8,128)S(1)}, u32[]{:S(2)}, u32[]{:S(2)}) collective-permute-start(f32[5,256]{0,1:T(8,128)S(1)} %bitcast.497), channel_id=1, source_target_pairs={{32,0},{64,32},{96,64},{128,96},{160,128},{192,160},{224,192},{33,... | collective-permute-start | bytes 15368 | tf_op jit(solution)/shard_map/ppermute | solution.py:13
  20.1 4.9 collective-permute-start
  33.7 104.0 %all-to-all-start = ((f32[32,5,4096]{2,1,0:T(8,128)}), f32[32,5,4096]{2,1,0:T(8,128)}, u32[]{:S(2)}, u32[]{:S(2)}) async-start(f32[32,5,4096]{2,1,0:T(8,128)} %stack.12), calls=%async_computation | async-start | bytes 8388608 | tf_op jit(solution)/shard_map/all_to_all | solution.py:94
  57.7 39.0 %copy-start.39 = (s32[32,128]{1,0:T(8,128)S(1)}, s32[32,128]{1,0:T(8,128)}, u32[]{:S(2)}) copy-start(s32[32,128]{1,0:T(8,128)} %param.25) | copy-start | bytes 49156
  137.6 30.6 %copy-start.30 = (s32[4096]{0:T(1024)}, s32[4096]{0:T(1024)S(1)}, u32[]{:S(2)}) copy-start(s32[4096]{0:T(1024)S(1)} %broadcast_clamp_fusion) | copy-start | bytes 49156
  168.2 66.9 %copy-start.13 = (f32[5,5,128]{2,1,0:T(8,128)S(1)}, f32[5,5,128]{2,1,0:T(8,128)}, u32[]{:S(2)}) copy-start(f32[5,5,128]{2,1,0:T(8,128)} %reshape_squeeze.385) | copy-start | bytes 38404
  168.2 67.7 %copy-start.11 = (f32[5,5,128]{2,1,0:T(8,128)S(1)}, f32[5,5,128]{2,1,0:T(8,128)}, u32[]{:S(2)}) copy-start(f32[5,5,128]{2,1,0:T(8,128)} %reshape_squeeze.388) | copy-start | bytes 38404
  168.2 68.4 %copy-start.9 = (f32[5,5,128]{2,1,0:T(8,128)S(1)}, f32[5,5,128]{2,1,0:T(8,128)}, u32[]{:S(2)}) copy-start(f32[5,5,128]{2,1,0:T(8,128)} %reshape_squeeze.391) | copy-start | bytes 38404
  168.2 69.2 %copy-start.7 = (f32[5,5,128]{2,1,0:T(8,128)S(1)}, f32[5,5,128]{2,1,0:T(8,128)}, u32[]{:S(2)}) copy-start(f32[5,5,128]{2,1,0:T(8,128)} %reshape_squeeze.394) | copy-start | bytes 38404
  168.2 70.0 %copy-start.6 = (f32[5,5,128]{2,1,0:T(8,128)S(1)}, f32[5,5,128]{2,1,0:T(8,128)}, u32[]{:S(2)}) copy-start(f32[5,5,128]{2,1,0:T(8,128)} %reshape_squeeze.397) | copy-start | bytes 38404
  168.3 70.8 %copy-start.5 = (f32[5,5,128]{2,1,0:T(8,128)S(1)}, f32[5,5,128]{2,1,0:T(8,128)}, u32[]{:S(2)}) copy-start(f32[5,5,128]{2,1,0:T(8,128)} %reshape_squeeze.400) | copy-start | bytes 38404
  231.2 28.1 %copy-start.24 = (f32[5,5,128]{2,1,0:T(8,128)S(1)}, f32[5,5,128]{2,1,0:T(8,128)}, u32[]{:S(2)}) copy-start(f32[5,5,128]{2,1,0:T(8,128)} %reshape_squeeze.461) | copy-start | bytes 38404
  231.2 28.1 %copy-start.20 = (f32[5,5,128]{2,1,0:T(8,128)S(1)}, f32[5,5,128]{2,1,0:T(8,128)}, u32[]{:S(2)}) copy-start(f32[5,5,128]{2,1,0:T(8,128)} %reshape_squeeze.458) | copy-start | bytes 38404
  231.2 28.2 %copy-start.18 = (f32[5,5,128]{2,1,0:T(8,128)S(1)}, f32[5,5,128]{2,1,0:T(8,128)}, u32[]{:S(2)}) copy-start(f32[5,5,128]{2,1,0:T(8,128)} %reshape_squeeze.455) | copy-start | bytes 38404
  231.3 28.2 %copy-start.16 = (f32[5,5,128]{2,1,0:T(8,128)S(1)}, f32[5,5,128]{2,1,0:T(8,128)}, u32[]{:S(2)}) copy-start(f32[5,5,128]{2,1,0:T(8,128)} %reshape_squeeze.452) | copy-start | bytes 38404
  319.8 13.8 %collective-permute-start.3 = (f32[5,256]{0,1:T(8,128)}, f32[5,256]{0,1:T(8,128)}, u32[]{:S(2)}, u32[]{:S(2)}) collective-permute-start(f32[5,256]{0,1:T(8,128)} %bitcast.498), channel_id=1, source_target_pairs={{32,0},{64,32},{96,64},{128,96},{160,128},{192,160},{224,192},{33,... | collective-permute-start | bytes 15368 | tf_op jit(solution)/shard_map/ppermute | solution.py:13
  321.9 8.5 %collective-permute-start.2 = (f32[5,256]{0,1:T(8,128)}, f32[5,256]{0,1:T(8,128)}, u32[]{:S(2)}, u32[]{:S(2)}) collective-permute-start(f32[5,256]{0,1:T(8,128)} %bitcast.500), channel_id=1, source_target_pairs={{0,32},{32,64},{64,96},{96,128},{128,160},{160,192},{192,224},{1,3... | collective-permute-start | bytes 15368 | tf_op jit(solution)/shard_map/ppermute | solution.py:13
  339.8 98.0 %all-to-all-start.3 = ((f32[32,5,4096]{2,1,0:T(8,128)}), f32[32,5,4096]{2,1,0:T(8,128)}, u32[]{:S(2)}, u32[]{:S(2)}) async-start(f32[32,5,4096]{2,1,0:T(8,128)} %stack.15), calls=%async_computation.3 | async-start | bytes 8388608 | tf_op jit(solution)/shard_map/all_to_all | solution.py:94
  437.9 30.6 %copy-start.31 = (s32[4096]{0:T(1024)S(1)}, s32[4096]{0:T(1024)}, u32[]{:S(2)}) copy-start(s32[4096]{0:T(1024)} %copy-done.30) | copy-start | bytes 49156
  531.4 28.1 %copy-start.19 = (f32[5,5,128]{2,1,0:T(8,128)S(1)}, f32[5,5,128]{2,1,0:T(8,128)}, u32[]{:S(2)}) copy-start(f32[5,5,128]{2,1,0:T(8,128)} %reshape_squeeze.455) | copy-start | bytes 38404
  531.4 28.1 %copy-start.17 = (f32[5,5,128]{2,1,0:T(8,128)S(1)}, f32[5,5,128]{2,1,0:T(8,128)}, u32[]{:S(2)}) copy-start(f32[5,5,128]{2,1,0:T(8,128)} %reshape_squeeze.452) | copy-start | bytes 38404
  613.3 15.2 %collective-permute-start.5 = (f32[5,256]{0,1:T(8,128)S(1)}, f32[5,256]{0,1:T(8,128)S(1)}, u32[]{:S(2)}, u32[]{:S(2)}) collective-permute-start(f32[5,256]{0,1:T(8,128)S(1)} %bitcast.496), channel_id=1, source_target_pairs={{32,0},{64,32},{96,64},{128,96},{160,128},{192,160},{224,192},{33,... | collective-permute-start | bytes 15368 | tf_op jit(solution)/shard_map/ppermute | solution.py:13
  615.6 9.7 %collective-permute-start.4 = (f32[5,256]{0,1:T(8,128)S(1)}, f32[5,256]{0,1:T(8,128)S(1)}, u32[]{:S(2)}, u32[]{:S(2)}) collective-permute-start(f32[5,256]{0,1:T(8,128)S(1)} %bitcast.499), channel_id=1, source_target_pairs={{0,32},{32,64},{64,96},{96,128},{128,160},{160,192},{192,224},{1,3... | collective-permute-start | bytes 15368 | tf_op jit(solution)/shard_map/ppermute | solution.py:13
  (31 other events, 580.3 us)
